TPU v7x, 32 devices: a whole 2x2x4 slice. The times are simulated.
32 devices in a mesh: row: 4 (over z), col: 8 (over y, x, core).
Axes of the slice: x: 2, y: 2, z: 4, core: 2. Of those that a mesh axis runs over, the one named last changes fastest.
Arguments:
- inverse_top: bfloat16 [1024, 1024], P('col', 'row'), may hold values from -0.1875 to 0.1875
- inverse_one: bfloat16 [1536, 768], P('col', 'row'), may hold values from -0.21875 to 0.21875
- inverse_two: bfloat16 [2048, 512], P('col', 'row'), may hold values from -0.25 to 0.25
- inverse_leaf: bfloat16 [2048, 256], P('col', 'row'), may hold values from -0.375 to 0.375
- coupling_one: bfloat16 [768, 1536], P('row', 'col'), may hold values from -0.21875 to 0.21875
- coupling_two: bfloat16 [512, 2048], P('row', 'col'), may hold values from -0.25 to 0.25
- coupling_leaf: bfloat16 [256, 2048], P('row', 'col'), may hold values from -0.375 to 0.375
- rhs_top: bfloat16 [1024, 256], P('row', 'col'), may hold values from -6 to 6
- rhs_one: bfloat16 [768, 512], P('row', 'col'), may hold values from -6 to 6
- rhs_two: bfloat16 [512, 1024], P('row', 'col'), may hold values from -6 to 6
- rhs_leaf: bfloat16 [256, 2048], P('row', 'col'), may hold values from -6 to 6
- parent_map_one: int32 [2, 768], replicated, may hold values from 0 to 1023, as said below
- parent_map_two: int32 [4, 512], replicated, may hold values from 0 to 1535, as said below
- parent_map_leaf: int32 [8, 256], replicated, may hold values from 0 to 1023, as said below
Outputs:
- solution_top: bfloat16 [1024, 256], P('row', 'col')
- solution_one: bfloat16 [768, 512], P('row', 'col')
- solution_two: bfloat16 [512, 1024], P('row', 'col')
- solution_leaf: bfloat16 [256, 2048], P('row', 'col')
Inputs may be any that keep to these rules, and one draw needn't show every extreme that they name: `parent_map_one`: row k lists distinct rows of the top front, one for each of the 768 update rows of front k. Cut the update rows and the top separator each into 4 equal blocks: at most 96 rows of one block land in one block of the top front, a number that is reached in every row, and every block of the top front receives exactly 192 rows from each child. `parent_map_two`: row k lists distinct rows of the front k // 2 of the second level (its 768 separator rows first, then its 768 update rows), one for each of the 512 update rows of front k. Cut the update rows into 4 equal blocks, and the parent's separator rows and its update rows each into 4 equal blocks, block j of the parent being the j-th separator block with the j-th update block: at most 64 rows of one block land in one parent block, reached in every row, and every parent block receives exactly 128 rows from each child. `parent_map_leaf`: as for parent_map_two, one level lower: 256 update rows of front k into front k // 2 of the third level, at most 32 rows of one block into one parent block, reached in every row, and exactly 64 rows from each child into every parent block.
All inputs are finite; a program needn't handle non-finite values.
Results may differ from a plain program's by a relative error of at most 0.03.
Values may be sent and summed in bfloat16 or wider, within the bound.
A program may use at most 64 MiB of HBM per device.

v0:
```python
import jax
import jax.numpy as jnp
from jax import lax
from jax.sharding import PartitionSpec as P


def swapped(value, axis, stride):
    mask = 2**stride
    pairs = [(source, source ^ mask) for source in range(lax.axis_size(axis))]
    return lax.ppermute(value, axis, pairs)


def route_tables(mapping, child_index, parent_sep, parent_upd, strips, row_index):
    positions = lax.dynamic_index_in_dim(mapping, child_index, 0, keepdims=False)
    sep_rows = parent_sep // strips
    in_separator = positions < parent_sep
    if parent_upd > 0:
        upd_rows = parent_upd // strips
        target = jnp.where(
            in_separator, positions // sep_rows, (positions - parent_sep) // upd_rows
        )
        offset = jnp.where(
            in_separator, positions % sep_rows, sep_rows + (positions - parent_sep) % upd_rows
        )
    else:
        target = positions // sep_rows
        offset = positions % sep_rows
    block_rows = positions.shape[0] // strips
    blocks = target.reshape(strips, block_rows)
    matches = (blocks[:, :, None] == jnp.arange(strips, dtype=jnp.int32)[None, None, :]).astype(
        jnp.int32
    )
    slot_of = jnp.sum((jnp.cumsum(matches, axis=1) - 1) * matches, axis=2).reshape(-1)
    block_len = sep_rows + parent_upd // strips
    capacity = 2 * positions.shape[0] // (strips * strips)
    source = jnp.arange(positions.shape[0], dtype=jnp.int32) // block_rows
    mine_here = target == row_index
    column_at = jnp.where(mine_here, slot_of, capacity)
    lookup = jnp.full((strips, capacity + 1), block_len, jnp.int32)
    lookup = lookup.at[source, column_at].set(jnp.where(mine_here, offset, block_len))[:, :capacity]
    local_target = lax.dynamic_slice_in_dim(target, row_index * block_rows, block_rows)
    local_slots = lax.dynamic_slice_in_dim(slot_of, row_index * block_rows, block_rows)
    return (local_target, local_slots, lookup, capacity, block_len)


def pack_rows(values, local_target, local_slots, strips, capacity):
    buffer = jnp.zeros((strips, capacity, values.shape[1]), values.dtype)
    return buffer.at[local_target, local_slots].set(values)


def unpack_rows(received, lookup, block_len):
    summed = jnp.zeros((block_len + 1, received.shape[2]), jnp.float32)
    return summed.at[lookup].add(received.astype(jnp.float32))[:block_len]


def spread(portion, depth_bits, pass_on, column):
    for bit_index in range(depth_bits):
        partner = pass_on(portion, bit_index)
        is_upper = column >> bit_index & 1 == 1
        portion = jnp.where(
            is_upper,
            jnp.concatenate([partner, portion], axis=-1),
            jnp.concatenate([portion, partner], axis=-1),
        )
    return portion


def shrink(entire, depth_bits, pass_on, column):
    for bit_index in reversed(range(depth_bits)):
        half_width = entire.shape[-1] // 2
        low_part = entire[..., :half_width]
        high_part = entire[..., half_width:]
        is_upper = column >> bit_index & 1 == 1
        kept_part = jnp.where(is_upper, high_part, low_part)
        sent_part = jnp.where(is_upper, low_part, high_part)
        entire = kept_part + pass_on(sent_part, bit_index)
    return entire


def per_device(
    inverse_top,
    inverse_one,
    inverse_two,
    inverse_leaf,
    coupling_one,
    coupling_two,
    coupling_leaf,
    rhs_top,
    rhs_one,
    rhs_two,
    rhs_leaf,
    parent_map_one,
    parent_map_two,
    parent_map_leaf,
):
    strips = lax.axis_size("row")
    col_count = lax.axis_size("col")
    row_here = lax.axis_index("row")
    column = lax.axis_index("col")
    inverses = [inverse_top, inverse_one, inverse_two, inverse_leaf]
    couplings = [None, coupling_one, coupling_two, coupling_leaf]
    right_sides = [rhs_top, rhs_one, rhs_two, rhs_leaf]
    parent_maps = [None, parent_map_one, parent_map_two, parent_map_leaf]
    orders = [inverse.shape[1] * strips for inverse in inverses]
    groups = [col_count >> tree_level for tree_level in range(4)]
    group_bits = [group_size.bit_length() - 1 for group_size in groups]
    pass_rhs = lambda values, bit_index: swapped(values, "col", bit_index)
    pass_update_sum = lambda values, bit_index: swapped(
        values.astype(jnp.bfloat16), "col", bit_index
    ).astype(values.dtype)
    pass_update_spread = lambda values, bit_index: swapped(values, "col", bit_index)
    pass_solution_sum = lambda values, bit_index: swapped(
        values.astype(jnp.bfloat16), "col", bit_index
    ).astype(values.dtype)
    pass_solution_spread = lambda values, bit_index: swapped(values, "col", bit_index)
    full_rhs = [
        spread(right_sides[tree_level], group_bits[tree_level], pass_rhs, column)
        for tree_level in range(4)
    ]
    own_routes = [None]
    for tree_level in range(1, 4):
        parent_order = orders[tree_level - 1]
        parent_update = parent_order if tree_level > 1 else 0
        front_here = column // groups[tree_level]
        own_routes.append(
            route_tables(
                parent_maps[tree_level], front_here, parent_order, parent_update, strips, row_here
            )
        )
    pivots = [None] * 4
    incoming = None
    for tree_level in (3, 2, 1, 0):
        sep_rows = inverses[tree_level].shape[1]
        if incoming is None:
            separator = full_rhs[tree_level]
            own_update = None
        else:
            separator = (full_rhs[tree_level].astype(jnp.float32) + incoming[:sep_rows]).astype(
                jnp.bfloat16
            )
            own_update = lax.optimization_barrier(incoming[sep_rows:].astype(jnp.bfloat16))
        partial_value = jnp.dot(inverses[tree_level], separator, preferred_element_type=jnp.float32)
        solved = lax.psum(partial_value.astype(jnp.bfloat16), "row")
        pivots[tree_level] = solved
        if tree_level > 0:
            coupled = jnp.dot(couplings[tree_level], solved, preferred_element_type=jnp.float32)
            reduced = shrink(coupled, group_bits[tree_level], pass_update_sum, column)
            if own_update is None:
                portion = (-reduced).astype(jnp.bfloat16)
            else:
                start_at = column % groups[tree_level] * reduced.shape[1]
                kept_rows = lax.dynamic_slice_in_dim(own_update, start_at, reduced.shape[1], 1)
                portion = (kept_rows.astype(jnp.float32) - reduced).astype(jnp.bfloat16)
            updated = spread(portion, group_bits[tree_level], pass_update_spread, column)
            own_target, own_slots, own_lookup, capacity, block_len = own_routes[tree_level]
            got_own = lax.all_to_all(
                pack_rows(updated, own_target, own_slots, strips, capacity),
                "row",
                split_axis=0,
                concat_axis=0,
                tiled=True,
            )
            own_part = unpack_rows(got_own, own_lookup, block_len)
            partner = swapped(own_part.astype(jnp.bfloat16), "col", group_bits[tree_level])
            incoming = own_part + partner.astype(jnp.float32)
    solutions = [None] * 4
    parent_solution = None
    parent_gathered = None
    for tree_level in range(4):
        solved = pivots[tree_level]
        gathered = None
        if tree_level == 0:
            residual = solved
        else:
            own_target, own_slots, own_lookup, capacity, block_len = own_routes[tree_level]
            pieces = [parent_solution]
            if parent_gathered is not None:
                pieces.append(parent_gathered)
            pieces.append(jnp.zeros((1, parent_solution.shape[1]), jnp.bfloat16))
            parent_rows = jnp.concatenate(pieces, axis=0)
            returned = lax.all_to_all(
                parent_rows[own_lookup], "row", split_axis=0, concat_axis=0, tiled=True
            )
            gathered = returned[own_target, own_slots]
            coupling_term = jnp.dot(
                couplings[tree_level].T, gathered, preferred_element_type=jnp.float32
            )
            residual = (
                solved.astype(jnp.float32)
                - lax.psum(coupling_term.astype(jnp.bfloat16), "row").astype(jnp.float32)
            ).astype(jnp.bfloat16)
        contribution = jnp.dot(inverses[tree_level].T, residual, preferred_element_type=jnp.float32)
        if tree_level == 0:
            summed = lax.psum(contribution.astype(jnp.bfloat16), "col")
            solution = summed
            rhs_width = solution.shape[1] // groups[0]
            solutions[0] = lax.dynamic_slice_in_dim(
                solution, column % groups[0] * rhs_width, rhs_width, 1
            )
        else:
            portion = shrink(
                contribution, group_bits[tree_level], pass_solution_sum, column
            ).astype(jnp.bfloat16)
            solutions[tree_level] = portion
            if tree_level < 3:
                solution = spread(portion, group_bits[tree_level], pass_solution_spread, column)
        parent_solution = solution
        parent_gathered = gathered
    return (solutions[0], solutions[1], solutions[2], solutions[3])


def solution(mesh):
    in_specs = (
        P("col", "row"),
        P("col", "row"),
        P("col", "row"),
        P("col", "row"),
        P("row", "col"),
        P("row", "col"),
        P("row", "col"),
        P("row", "col"),
        P("row", "col"),
        P("row", "col"),
        P("row", "col"),
        P(),
        P(),
        P(),
    )
    out_specs = (P("row", "col"), P("row", "col"), P("row", "col"), P("row", "col"))
    return jax.shard_map(
        per_device, mesh=mesh, in_specs=in_specs, out_specs=out_specs, check_vma=False
    )
```

profile of v0, /device:TPU:0, one launch (start us, length us, event | category | flops | bytes accessed | tf_op | source)
XLA Modules:
  0.0 545.7 jit_solution(7901075325292070809)
XLA Ops:
  16.1 11.5 %scatter_fusion.2 = s32[4,33]{1,0:T(4,128)S(1)} fusion(s32[4,33]{1,0:T(4,128)S(1)} %broadcast_in_dim.99, s32[256]{0:T(256)S(1)} %bitcast.176, s32[256]{0:T(256)S(1)} %get-tuple-element.17), kind=kCustom, calls=%fused_computation.8 | custom fusion | bytes 5120 | tf_op jit(solution)/shard_map/scatter | solution.py:40
  27.6 20.1 %all-reduce.11.cloned.1.call-done = bf16[256,256]{1,0:T(8,128)(2,1)} async-done(((bf16[256,256]{1,0:T(8,128)(2,1)}), bf16[256,256]{1,0:T(8,128)(2,1)}) %all-reduce.11.cloned.1.call-update) | async-done | bytes 131088 | tf_op jit(solution)/shard_map/psum | solution.py:143
  49.4 8.2 %scatter_fusion.3 = bf16[4,32,256]{2,1,0:T(8,128)(2,1)} fusion(bf16[4,32,256]{2,1,0:T(8,128)(2,1)} %broadcast_in_dim.103, s32[64]{0:T(128)S(1)} %get-tuple-element.30, bf16[64,256]{1,0:T(8,128)(2,1)S(1)} %fusion.9), kind=kCustom, calls=%fused_computation.9 | custom fusion | bytes 98816 | tf_op jit(solution)/shard_map/scatter | solution.py:48
  57.6 3.5 all-to-all-start
  61.2 22.5 %scatter_fusion.1 = s32[4,65]{1,0:T(4,128)S(1)} fusion(s32[4,65]{1,0:T(4,128)S(1)} %broadcast_in_dim.92, s32[512]{0:T(512)S(1)} %bitcast.175, s32[512]{0:T(512)S(1)} %get-tuple-element.21), kind=kCustom, calls=%fused_computation.7 | custom fusion | bytes 10240 | tf_op jit(solution)/shard_map/scatter | solution.py:40
  87.7 36.1 %all-reduce.13.cloned.1.call-done = bf16[256,256]{0,1:T(8,128)(2,1)} async-done(((bf16[256,256]{0,1:T(8,128)(2,1)}), bf16[256,256]{0,1:T(8,128)(2,1)}) %all-reduce.13.cloned.1.call-update) | async-done | bytes 131088 | tf_op jit(solution)/shard_map/psum | solution.py:143
  126.6 4.8 reduce-window.6
  132.5 15.8 %scatter_fusion.4 = bf16[4,64,256]{2,1,0:T(8,128)(2,1)} fusion(bf16[4,64,256]{2,1,0:T(8,128)(2,1)} %broadcast_in_dim.96, s32[128]{0:T(128)S(1)} %get-tuple-element.26, bf16[128,256]{1,0:T(8,128)(2,1)S(1)} %copy.42), kind=kCustom, calls=%fused_computation.11 | custom fusion | bytes 197632 | tf_op jit(solution)/shard_map/scatter | solution.py:48
  148.2 3.3 all-to-all-start.1
  151.8 6.3 %all-to-all-done.1 = bf16[4,64,256]{2,1,0:T(8,128)(2,1)S(1)} async-done(((bf16[4,64,256]{2,1,0:T(8,128)(2,1)}), bf16[4,64,256]{2,1,0:T(8,128)(2,1)S(1)}, u32[]{:S(2)}, u32[]{:S(2)}) %all-to-all-start.1) | async-done | bytes 131104 | tf_op jit(solution)/shard_map/all_to_all | solution.py:156
  158.0 2.2 scatter_custom_fusion.6
  162.6 3.7 collective-permute-done.7
  167.8 34.7 %all-reduce.15.cloned.1.call-done = bf16[192,256]{1,0:T(8,128)(2,1)} async-done(((bf16[192,256]{1,0:T(8,128)(2,1)}), bf16[192,256]{1,0:T(8,128)(2,1)}) %all-reduce.15.cloned.1.call-update) | async-done | bytes 98320 | tf_op jit(solution)/shard_map/psum | solution.py:143
  205.2 2.5 collective-permute-done.10
  212.3 33.5 %scatter_fusion = s32[4,97]{1,0:T(4,128)S(1)} fusion(s32[4,97]{1,0:T(4,128)S(1)} %broadcast_in_dim.85, s32[768]{0:T(1024)S(1)} %fusion.52, s32[768]{0:T(1024)S(1)} %get-tuple-element.28), kind=kCustom, calls=%fused_computation.6 | custom fusion | bytes 15360 | tf_op jit(solution)/shard_map/scatter | solution.py:40
  246.6 23.9 %scatter_fusion.5 = bf16[4,96,256]{2,1,0:T(8,128)(2,1)} fusion(bf16[4,96,256]{2,1,0:T(8,128)(2,1)} %broadcast_in_dim.88, s32[192]{0:T(256)S(1)} %bitcast.177, bf16[192,256]{1,0:T(8,128)(2,1)S(1)} %maximum_select_fusion.4), kind=kCustom, calls=%fused_computation.13 | custom fusion | bytes 296448 | tf_op jit(solution)/shard_map/scatter | solution.py:48
  270.5 3.4 all-to-all-start.2
  274.9 6.7 %all-to-all-done.2 = bf16[4,96,256]{2,1,0:T(8,128)(2,1)S(1)} async-done(((bf16[4,96,256]{2,1,0:T(8,128)(2,1)}), bf16[4,96,256]{2,1,0:T(8,128)(2,1)S(1)}, u32[]{:S(2)}, u32[]{:S(2)}) %all-to-all-start.2) | async-done | bytes 196640 | tf_op jit(solution)/shard_map/all_to_all | solution.py:156
  281.7 2.9 scatter_custom_fusion.8
  286.9 3.7 collective-permute-done.2
  291.6 32.7 %all-reduce.17.cloned.1.call-done = bf16[128,256]{0,1:T(8,128)(2,1)} async-done(((bf16[128,256]{0,1:T(8,128)(2,1)}), bf16[128,256]{0,1:T(8,128)(2,1)}) %all-reduce.17.cloned.1.call-update) | async-done | bytes 65552 | tf_op jit(solution)/shard_map/psum | solution.py:143
  326.0 54.3 %all-reduce.19.cloned.1.call-done = bf16[256,256]{0,1:T(8,128)(2,1)} async-done(((bf16[256,256]{0,1:T(8,128)(2,1)}), bf16[256,256]{0,1:T(8,128)(2,1)}) %all-reduce.19.cloned.1.call-update) | async-done | bytes 131088 | tf_op jit(solution)/shard_map/psum | solution.py:194
  381.4 2.1 gather_fusion
  383.4 11.2 %all_to_all.30 = bf16[4,96,256]{2,1,0:T(8,128)(2,1)S(1)} all-to-all(bf16[4,96,256]{2,1,0:T(8,128)(2,1)S(1)} %bitcast.180), channel_id=1, replica_groups=mesh['row'=4,'col'=8] {'row'}, dimensions={0} | all-to-all | bytes 393216 | tf_op jit(solution)/shard_map/all_to_all | solution.py:181
  394.6 2.4 gather_fusion.1
  398.0 31.9 %all-reduce.21.cloned.1.call-done = bf16[192,256]{1,0:T(8,128)(2,1)} async-done(((bf16[192,256]{1,0:T(8,128)(2,1)}), bf16[192,256]{1,0:T(8,128)(2,1)}) %all-reduce.21.cloned.1.call-update) | async-done | bytes 98320 | tf_op jit(solution)/shard_map/psum | solution.py:190
  432.6 2.6 collective-permute-done.15
  439.7 2.6 collective-permute-done.18
  443.6 9.1 %all_to_all.31 = bf16[4,64,256]{2,1,0:T(8,128)(2,1)S(1)} all-to-all(bf16[4,64,256]{2,1,0:T(8,128)(2,1)S(1)} %bitcast.182), channel_id=1, replica_groups=mesh['row'=4,'col'=8] {'row'}, dimensions={0} | all-to-all | bytes 262144 | tf_op jit(solution)/shard_map/all_to_all | solution.py:181
  454.8 33.7 %all-reduce.23.cloned.1.call-done = bf16[256,256]{0,1:T(8,128)(2,1)} async-done(((bf16[256,256]{0,1:T(8,128)(2,1)}), bf16[256,256]{0,1:T(8,128)(2,1)}) %all-reduce.23.cloned.1.call-update) | async-done | bytes 131088 | tf_op jit(solution)/shard_map/psum | solution.py:190
  493.2 8.9 %all_to_all.32 = bf16[4,32,256]{2,1,0:T(8,128)(2,1)S(1)} all-to-all(bf16[4,32,256]{2,1,0:T(8,128)(2,1)S(1)} %bitcast.183), channel_id=1, replica_groups=mesh['row'=4,'col'=8] {'row'}, dimensions={0} | all-to-all | bytes 131072 | tf_op jit(solution)/shard_map/all_to_all | solution.py:181
  506.7 30.5 %all-reduce.25.cloned.1.call-done = bf16[256,256]{1,0:T(8,128)(2,1)} async-done(((bf16[256,256]{1,0:T(8,128)(2,1)}), bf16[256,256]{1,0:T(8,128)(2,1)}) %all-reduce.25.cloned.1.call-update) | async-done | bytes 131088 | tf_op jit(solution)/shard_map/psum | solution.py:190
  (203 shorter events, 59.2 us)
Async XLA Ops:
  7.2 40.5 %all-reduce.11.cloned.1.call-start = ((), (), s32[]{:S(2)}) async-start(), calls=%async_computation.6 | async-start | bytes 262144 | tf_op jit(solution)/shard_map/psum | solution.py:143
  9.8 77.0 %collective-permute-start.4 = (bf16[128,128]{0,1:T(8,128)(2,1)S(1)}, bf16[128,128]{0,1:T(8,128)(2,1)S(1)}, u32[]{:S(2)}, u32[]{:S(2)}) collective-permute-start(bf16[128,128]{0,1:T(8,128)(2,1)S(1)} %copy.39), channel_id=1, source_target_pairs={{0,1},{1,0},{2,3},{3,2},{4,5},{5,4},{6,7},{7,6},{8,9},{9,8},{10,11... | collective-permute-start | bytes 98312 | tf_op jit(solution)/shard_map/ppermute | solution.py:10
  10.5 151.6 %collective-permute-start.8 = (bf16[192,64]{1,0:T(8,128)(2,1)S(1)}, bf16[192,64]{1,0:T(8,128)(2,1)S(1)}, u32[]{:S(2)}, u32[]{:S(2)}) collective-permute-start(bf16[192,64]{1,0:T(8,128)(2,1)S(1)} %copy.43), channel_id=1, source_target_pairs={{0,1},{1,0},{2,3},{3,2},{4,5},{5,4},{6,7},{7,6},{8,9},{9,8},{10,11... | collective-permute-start | bytes 73736 | tf_op jit(solution)/shard_map/ppermute | solution.py:10
  11.2 262.9 %collective-permute-start = (bf16[256,32]{1,0:T(8,128)(2,1)S(1)}, bf16[256,32]{1,0:T(8,128)(2,1)S(1)}, u32[]{:S(2)}, u32[]{:S(2)}) collective-permute-start(bf16[256,32]{1,0:T(8,128)(2,1)S(1)} %copy.33), channel_id=1, source_target_pairs={{0,1},{1,0},{2,3},{3,2},{4,5},{5,4},{6,7},{7,6},{8,9},{9,8},{10,11... | collective-permute-start | bytes 49160 | tf_op jit(solution)/shard_map/ppermute | solution.py:10
  57.6 26.2 %all-to-all-start = ((bf16[4,32,256]{2,1,0:T(8,128)(2,1)}), bf16[4,32,256]{2,1,0:T(8,128)(2,1)S(1)}, u32[]{:S(2)}, u32[]{:S(2)}) async-start(bf16[4,32,256]{2,1,0:T(8,128)(2,1)} %scatter_fusion.3), calls=%async_computation | async-start | bytes 131072 | tf_op jit(solution)/shard_map/all_to_all | solution.py:156
  61.1 62.7 %all-reduce.13.cloned.1.call-start = ((), (), s32[]{:S(2)}) async-start(), calls=%async_computation.7 | async-start | bytes 262144 | tf_op jit(solution)/shard_map/psum | solution.py:143
  85.3 1.4 collective-permute-start.3
  124.9 1.3 collective-permute-start.5
  126.2 5.5 %collective-permute-start.6 = (bf16[128,128]{0,1:T(8,128)(2,1)S(1)}, bf16[128,128]{0,1:T(8,128)(2,1)S(1)}, u32[]{:S(2)}, u32[]{:S(2)}) collective-permute-start(bf16[128,128]{0,1:T(8,128)(2,1)S(1)} %subtract_convert_fusion.7), channel_id=1, source_target_pairs={{0,1},{1,0},{2,3},{3,2},{4,5},{5,4},{6,7},{7,6},{8,9},{9,8},{10,11... | collective-permute-start | bytes 98312 | tf_op jit(solution)/shard_map/ppermute | solution.py:10
  148.2 9.8 %all-to-all-start.1 = ((bf16[4,64,256]{2,1,0:T(8,128)(2,1)}), bf16[4,64,256]{2,1,0:T(8,128)(2,1)S(1)}, u32[]{:S(2)}, u32[]{:S(2)}) async-start(bf16[4,64,256]{2,1,0:T(8,128)(2,1)} %scatter_fusion.4), calls=%async_computation.1 | async-start | bytes 262144 | tf_op jit(solution)/shard_map/all_to_all | solution.py:156
  151.6 51.0 %all-reduce.15.cloned.1.call-start = ((), (), s32[]{:S(2)}) async-start(), calls=%async_computation.8 | async-start | bytes 196608 | tf_op jit(solution)/shard_map/psum | solution.py:143
  160.3 6.1 %collective-permute-start.7 = (bf16[384,256]{1,0:T(8,128)(2,1)S(1)}, bf16[384,256]{1,0:T(8,128)(2,1)S(1)}, u32[]{:S(2)}, u32[]{:S(2)}) collective-permute-start(bf16[384,256]{1,0:T(8,128)(2,1)S(1)} %slice.195), channel_id=1, source_target_pairs={{0,2},{1,3},{2,0},{3,1},{4,6},{5,7},{6,4},{7,5},{8,10},{9,11},{10,... | collective-permute-start | bytes 589832 | tf_op jit(solution)/shard_map/ppermute | solution.py:10
  162.2 4.7 collective-permute-start.9
  203.6 4.2 collective-permute-start.10
  207.9 1.3 collective-permute-start.11
  209.3 1.3 collective-permute-start.12
  210.7 35.2 %collective-permute-start.13 = (bf16[192,128]{1,0:T(8,128)(2,1)S(1)}, bf16[192,128]{1,0:T(8,128)(2,1)S(1)}, u32[]{:S(2)}, u32[]{:S(2)}) collective-permute-start(bf16[192,128]{1,0:T(8,128)(2,1)S(1)} %maximum_select_fusion.13), channel_id=1, source_target_pairs={{0,2},{1,3},{2,0},{3,1},{4,6},{5,7},{6,4},{7,5},{8,10},{9,11},{10,... | collective-permute-start | bytes 147464 | tf_op jit(solution)/shard_map/ppermute | solution.py:10
  270.5 11.2 %all-to-all-start.2 = ((bf16[4,96,256]{2,1,0:T(8,128)(2,1)}), bf16[4,96,256]{2,1,0:T(8,128)(2,1)S(1)}, u32[]{:S(2)}, u32[]{:S(2)}) async-start(bf16[4,96,256]{2,1,0:T(8,128)(2,1)} %scatter_fusion.5), calls=%async_computation.2 | async-start | bytes 393216 | tf_op jit(solution)/shard_map/all_to_all | solution.py:156
  273.9 50.4 %all-reduce.17.cloned.1.call-start = ((), (), s32[]{:S(2)}) async-start(), calls=%async_computation.9 | async-start | bytes 131072 | tf_op jit(solution)/shard_map/psum | solution.py:143
  274.2 11.9 %collective-permute-start.1 = (bf16[256,64]{1,0:T(8,128)(2,1)S(1)}, bf16[256,64]{1,0:T(8,128)(2,1)S(1)}, u32[]{:S(2)}, u32[]{:S(2)}) collective-permute-start(bf16[256,64]{1,0:T(8,128)(2,1)S(1)} %maximum_select_fusion.6), channel_id=1, source_target_pairs={{0,2},{1,3},{2,0},{3,1},{4,6},{5,7},{6,4},{7,5},{8,10},{9,11},{10,... | collective-permute-start | bytes 98312 | tf_op jit(solution)/shard_map/ppermute | solution.py:10
  284.6 6.0 %collective-permute-start.14 = (bf16[256,256]{1,0:T(8,128)(2,1)S(1)}, bf16[256,256]{1,0:T(8,128)(2,1)S(1)}, u32[]{:S(2)}, u32[]{:S(2)}) collective-permute-start(bf16[256,256]{1,0:T(8,128)(2,1)S(1)} %slice.196), channel_id=1, source_target_pairs={{0,4},{1,5},{2,6},{3,7},{4,0},{5,1},{6,2},{7,3},{8,12},{9,13},{10,... | collective-permute-start | bytes 393224 | tf_op jit(solution)/shard_map/ppermute | solution.py:10
  286.3 4.3 collective-permute-start.2
  291.5 88.8 %all-reduce.19.cloned.1.call-start = ((), (), s32[]{:S(2)}) async-start(), calls=%async_computation.10 | async-start | bytes 262144 | tf_op jit(solution)/shard_map/psum | solution.py:194
  325.9 104.0 %all-reduce.21.cloned.1.call-start = ((), (), s32[]{:S(2)}) async-start(), calls=%async_computation.11 | async-start | bytes 196608 | tf_op jit(solution)/shard_map/psum | solution.py:190
  397.9 90.6 %all-reduce.23.cloned.1.call-start = ((), (), s32[]{:S(2)}) async-start(), calls=%async_computation.12 | async-start | bytes 262144 | tf_op jit(solution)/shard_map/psum | solution.py:190
  431.1 4.2 collective-permute-start.15
  435.3 1.3 collective-permute-start.16
  436.7 1.3 collective-permute-start.17
  438.1 4.2 collective-permute-start.18
  454.7 82.4 %all-reduce.25.cloned.1.call-start = ((), (), s32[]{:S(2)}) async-start(), calls=%async_computation.13 | async-start | bytes 262144 | tf_op jit(solution)/shard_map/psum | solution.py:190
  489.6 1.3 collective-permute-start.19
  490.9 1.3 collective-permute-start.20
  (14 other events, 409.0 us)
Sparse Core Ops, SparseCore 0:
  10.3 37.3 all-reduce.10
  87.8 35.9 all-reduce.12
  167.9 34.6 all-reduce.14
  291.6 32.5 all-reduce.16
  327.1 53.1 all-reduce.18
  398.0 31.8 all-reduce.20
  454.8 33.6 all-reduce.22
  504.0 33.1 all-reduce.24
where the time goes:
time: 548 us; the launch traced here: 546 us
  waiting for transfers between devices  312 us (57%)
  local copies, waits for them, and re-layouts  135 us (25%)
  blocking collectives  29.3 us (5%)
  starting transfers between devices  24.2 us (4%)
  matrix products  15.5 us (3%)
  other arithmetic  15.2 us (3%)
  between operations  14.9 us (3%)
    psum x4, waiting for transfers between devices, per_device(): solved = lax.psum(partial_value.astype(jnp.bfloat16), 'row')  124 us
    psum x3, waiting for transfers between devices, per_device(): lax.psum(coupling_term.astype(jnp.bfloat16), 'row').astype(jnp.float32)  96.1 us
    scatter x3, local copies, waits for them, and re-layouts, route_tables(): lookup.at[source, column_at].set(jnp.where(mine_here, offset, block_len))  67.5 us
    psum x1, waiting for transfers between devices, per_device(): summed = lax.psum(contribution.astype(jnp.bfloat16), 'col')  54.3 us
    scatter x3, local copies, waits for them, and re-layouts, pack_rows(): return buffer.at[local_target, local_slots].set(values)  47.9 us
    all_to_all x3, blocking collectives, per_device(): lax.all_to_all(parent_rows[own_lookup], 'row', split_axis=0, concat_axis=...  29.3 us
    ppermute x21, waiting for transfers between devices, swapped(): return lax.ppermute(value, axis, pairs)  24.6 us
    ppermute x21, starting transfers between devices, swapped(): return lax.ppermute(value, axis, pairs)  13.5 us
  transfers between devices with their start and end apart: 32, of which 24 were waited for; matrix products, arithmetic and copies ran while one was open for 26% of the time, Pallas kernels for 0%

commit v1 on v0

--- a/solution.py
+++ b/solution.py
@@ -1,6 +1,8 @@
 import jax
 import jax.numpy as jnp
 from jax import lax
+from jax.experimental import pallas as pl
+from jax.experimental.pallas import tpu as pltpu
 from jax.sharding import PartitionSpec as P
 
 
@@ -209,6 +211,463 @@
     return (solutions[0], solutions[1], solutions[2], solutions[3])
 
 
+MESH = pl.DeviceIdType.MESH
+
+
+def dot_nn(left, right):
+    return lax.dot_general(left, right, (((1,), (0,)), ((), ())), preferred_element_type=jnp.float32)
+
+
+def dot_nt(left, right):
+    return lax.dot_general(left, right, (((1,), (1,)), ((), ())), preferred_element_type=jnp.float32)
+
+
+def eye(size):
+    rows = lax.broadcasted_iota(jnp.int32, (size, size), 0)
+    columns = lax.broadcasted_iota(jnp.int32, (size, size), 1)
+    return jnp.where(rows == columns, 1.0, 0.0).astype(jnp.bfloat16)
+
+
+def flipped(value, mask):
+    result = value
+    bit = 1
+    while bit <= mask:
+        if mask & bit:
+            result = result + bit * (1 - 2 * ((value // bit) % 2))
+        bit *= 2
+    return result
+
+
+class Plan:
+    def __init__(self, rows, cols, inverse_shapes, rhs_top_shape):
+        self.rows, self.cols = rows, cols
+        self.strip = [shape[1] for shape in inverse_shapes]
+        self.order = [shape[1] * rows for shape in inverse_shapes]
+        self.local = [shape[0] for shape in inverse_shapes]
+        self.group = [cols >> level for level in range(4)]
+        self.columns = rhs_top_shape[1] * cols
+        self.width = [self.columns // group if group else 0 for group in self.group]
+        self.mine = self.columns // rows
+
+    def total(self, level):
+        return self.order[level] * (2 if level else 1)
+
+    def fits(self):
+        table = sum(
+            2 * self.total(level) * self.order[level + 1] * 2 for level in range(3)
+        )
+        if self.group[3] != 1 or self.mine * self.rows != self.columns or table > 24 * 2**20:
+            return False
+        for level in range(4):
+            if self.strip[level] % 16 or self.order[level] % 128 or self.width[level] % 16:
+                return False
+            if max(self.width[level], self.mine) % min(self.width[level], self.mine):
+                return False
+        for level in (1, 2):
+            if self.mine % (16 * self.group[level]):
+                return False
+        return self.order[0] % (128 * self.group[0]) == 0 and self.group[0] % self.rows == 0
+
+
+def build_kernel(plan):
+    R, CC, N = plan.rows, plan.cols, plan.mine
+    S, K, L, G, W = plan.order, plan.strip, plan.local, plan.group, plan.width
+    bf = jnp.bfloat16
+    scratch, names = [], {}
+
+    def ref(name, shape, dtype=bf):
+        names[name] = len(scratch)
+        scratch.append(pltpu.VMEM(shape, dtype))
+
+    def sems(name, shape):
+        names[name] = len(scratch)
+        scratch.append(pltpu.SemaphoreType.DMA(shape))
+
+    for l in range(4):
+        n_dest = max(1, W[l] // N)
+        n_part = max(1, N // W[l])
+        ref(f"Z{l}", (R, L[l], K[l]))
+        sems(f"Zs{l}", (R,))
+        sems(f"Zr{l}", (R,))
+        if l:
+            ref(f"C{l}", (S[l], L[l]))
+            sems(f"Cs{l}", (R,))
+            sems(f"Cr{l}", (R,))
+        ref(f"bT{l}", (W[l], K[l]))
+        ref(f"B{l}", (R, N, K[l]))
+        sems(f"Bs{l}", (n_dest, G[l]))
+        sems(f"Br{l}", (R, n_part))
+        ref(f"y{l}", (N, L[l]))
+        ref(f"fx{l}", (R, N, K[l]))
+        ref(f"oT{l}", (W[l], K[l]))
+        sems(f"Os{l}", (R,))
+        sems(f"Or{l}", (n_dest,))
+        if l < 3:
+            ref(f"hot{l}", (2, plan.total(l), S[l + 1]))
+            if l:
+                shape = (G[l], R, N // G[l], K[l])
+                ref(f"xp{l}", shape)
+                ref(f"xr{l}", shape)
+                ref(f"xs{l}", shape)
+            else:
+                shape = (G[0], N, S[0] // G[0])
+                ref("xp0", shape)
+                ref("xr0", shape)
+                ref("xs0", shape)
+            for tag in ("xps", "xpr", "xss", "xsr"):
+                sems(f"{tag}{l}", (G[l],))
+        if l:
+            shape = (G[l], N // G[l], S[l])
+            ref(f"u{l}", (2,) + shape)
+            sems(f"us{l}", (2 * G[l],))
+            sems(f"ur{l}", (2 * G[l],))
+            ref(f"v{l}", (N, S[l]))
+            if G[l] > 1:
+                ref(f"H{l}", shape)
+                ref(f"up{l}", shape)
+                ref(f"ut{l}", shape)
+                sems(f"ups{l}", (G[l],))
+                sems(f"upr{l}", (G[l],))
+
+    def kernel(*refs):
+        inverse = refs[0:4]
+        coupling = (None,) + tuple(refs[4:7])
+        rhs = refs[7:11]
+        maps = (None,) + tuple(refs[11:14])
+        outs = refs[14:18]
+        held = refs[18:]
+        at = lambda name: held[names[name]]
+        z = lax.axis_index("row")
+        c = lax.axis_index("col")
+        sent = []
+
+        def remote(src, dst, ssem, rsem, z_to, c_to):
+            return pltpu.make_async_remote_copy(
+                src_ref=src, dst_ref=dst, send_sem=ssem, recv_sem=rsem,
+                device_id=(z_to, c_to), device_id_type=MESH,
+            )
+
+        def send(src, dst, ssem, rsem, z_to, c_to):
+            copy = remote(src, dst, ssem, rsem, z_to, c_to)
+            copy.start()
+            sent.append(copy.wait_send)
+
+        def send_or_copy(src, dst, ssem, rsem, z_to, c_to, here):
+            @pl.when(here)
+            def _():
+                pltpu.make_async_copy(src, dst, rsem).start()
+
+            @pl.when(jnp.logical_not(here))
+            def _():
+                remote(src, dst, ssem, rsem, z_to, c_to).start()
+
+            def finish():
+                @pl.when(jnp.logical_not(here))
+                def _():
+                    remote(src, dst, ssem, rsem, z_to, c_to).wait_send()
+
+            sent.append(finish)
+
+        def arrived(dst, rsem):
+            pltpu.make_async_copy(dst, dst, rsem).wait()
+
+        barrier = pltpu.get_barrier_semaphore()
+        for dz in range(R):
+            for m in range(CC):
+                if dz or m:
+                    pl.semaphore_signal(
+                        barrier, inc=1, device_id=((z + dz) % R, flipped(c, m)),
+                        device_id_type=MESH,
+                    )
+        for l in range(4):
+            at(f"bT{l}")[...] = dot_nt(eye(W[l]), rhs[l][...]).astype(bf)
+        pl.semaphore_wait(barrier, R * CC - 1)
+
+        def start_rhs(l):
+            q = c % G[l]
+            n_dest, n_part = max(1, W[l] // N), max(1, N // W[l])
+            for i in range(n_dest):
+                if W[l] >= N:
+                    z_to = q * n_dest + i
+                    src = at(f"bT{l}").at[pl.ds(i * N, N)]
+                    dst = at(f"B{l}").at[z]
+                    part = 0
+                else:
+                    z_to = q // n_part
+                    part = q % n_part
+                    src = at(f"bT{l}")
+                    dst = at(f"B{l}").at[z, pl.ds(pl.multiple_of(part * W[l], W[l]), W[l])]
+                for m in range(G[l]):
+                    ssem, rsem = at(f"Bs{l}").at[i, m], at(f"Br{l}").at[z, part]
+                    if m:
+                        send(src, dst, ssem, rsem, z_to, flipped(c, m))
+                    else:
+                        send_or_copy(src, dst, ssem, rsem, z_to, c, z_to == z)
+
+        def wait_rhs(l):
+            n_part = max(1, N // W[l])
+            for s in range(R):
+                for part in range(n_part):
+                    if n_part > 1:
+                        dst = at(f"B{l}").at[s, pl.ds(part * W[l], W[l])]
+                    else:
+                        dst = at(f"B{l}").at[s]
+                    arrived(dst, at(f"Br{l}").at[s, part])
+
+        def c_rows(l, index):
+            return at(f"C{l}").at[pl.ds(pl.multiple_of(index * K[l], 16), K[l])]
+
+        def start_weights(l):
+            pltpu.make_async_copy(inverse[l], at(f"Z{l}").at[z], at(f"Zr{l}").at[0]).start()
+            if l:
+                pltpu.make_async_copy(coupling[l], c_rows(l, z), at(f"Cr{l}").at[0]).start()
+            for d in range(1, R):
+                z_to = (z + d) % R
+                send(inverse[l], at(f"Z{l}").at[z], at(f"Zs{l}").at[d], at(f"Zr{l}").at[d], z_to, c)
+                if l:
+                    send(coupling[l], c_rows(l, z), at(f"Cs{l}").at[d], at(f"Cr{l}").at[d], z_to, c)
+
+        def wait_inverse(l):
+            for d in range(R):
+                arrived(at(f"Z{l}").at[(z + R - d) % R], at(f"Zr{l}").at[d])
+
+        def wait_coupling(l):
+            for d in range(R):
+                arrived(c_rows(l, (z + R - d) % R), at(f"Cr{l}").at[d])
+
+        def scatter(name, l, landed, ssem, rsem):
+            q = c % G[l]
+            for m in range(1, G[l]):
+                send(
+                    at(name).at[flipped(q, m)], at(landed).at[m],
+                    at(ssem).at[m], at(rsem).at[m], z, flipped(c, m),
+                )
+
+        def total(name, l, landed, rsem):
+            value = at(name)[c % G[l]].astype(jnp.float32)
+            for m in range(1, G[l]):
+                arrived(at(landed).at[m], at(rsem).at[m])
+                value = value + at(landed)[m].astype(jnp.float32)
+            return value
+
+        def share_solution(l):
+            q = c % G[l]
+            here = at(f"xs{l}").at[q]
+            for m in range(1, G[l]):
+                send(here, here, at(f"xss{l}").at[m], at(f"xsr{l}").at[m], z, flipped(c, m))
+
+        def wait_solution(l):
+            q = c % G[l]
+            for m in range(1, G[l]):
+                arrived(at(f"xs{l}").at[flipped(q, m)], at(f"xsr{l}").at[m])
+
+        def share_update(l):
+            child, q = (c // G[l]) % 2, c % G[l]
+            here = at(f"u{l}").at[child, q]
+            for m in range(1, 2 * G[l]):
+                send(here, here, at(f"us{l}").at[m], at(f"ur{l}").at[m], z, flipped(c, m))
+
+        def wait_update(l):
+            for m in range(1, 2 * G[l]):
+                other = flipped(c, m)
+                arrived(
+                    at(f"u{l}").at[(other // G[l]) % 2, other % G[l]], at(f"ur{l}").at[m]
+                )
+
+        def make_table(l):
+            front = c // G[l]
+            step = K[l]
+            for child in range(2):
+                row = maps[l + 1][pl.ds(2 * front + child, 1), :]
+
+                def body(i, carry):
+                    start = pl.multiple_of(i * step, 16)
+                    at_row = lax.broadcasted_iota(jnp.int32, (step, S[l + 1]), 0) + start
+                    at(f"hot{l}")[child, pl.ds(start, step), :] = jnp.where(
+                        at_row == row, 1.0, 0.0
+                    ).astype(bf)
+                    return carry
+
+                lax.fori_loop(0, plan.total(l) // step, body, 0)
+
+        def start_out(l):
+            q = c % G[l]
+            n_dest, n_part = max(1, W[l] // N), max(1, N // W[l])
+            if W[l] >= N:
+                holds = z // n_dest == q
+                index = z % n_dest
+                dst = at(f"oT{l}").at[pl.ds(pl.multiple_of(index * N, N), N)]
+            else:
+                holds = q // n_part == z
+                index = 0
+                dst = at(f"oT{l}")
+
+            def piece(r):
+                if W[l] >= N:
+                    return at(f"fx{l}").at[r]
+                low = pl.multiple_of((q % n_part) * W[l], W[l])
+                return at(f"fx{l}").at[r, pl.ds(low, W[l])]
+
+            def copy_to(d):
+                r = (z + d) % R
+                return remote(
+                    piece(r), dst, at(f"Os{l}").at[d], at(f"Or{l}").at[index], r, c
+                )
+
+            @pl.when(holds)
+            def _():
+                pltpu.make_async_copy(piece(z), dst, at(f"Or{l}").at[index]).start()
+                for d in range(1, R):
+                    copy_to(d).start()
+
+            def finish():
+                @pl.when(holds)
+                def _():
+                    for d in range(1, R):
+                        copy_to(d).wait_send()
+
+            sent.append(finish)
+
+        def finish_out(l):
+            if W[l] >= N:
+                for i in range(W[l] // N):
+                    arrived(at(f"oT{l}").at[pl.ds(i * N, N)], at(f"Or{l}").at[i])
+            else:
+                arrived(at(f"oT{l}"), at(f"Or{l}").at[0])
+            outs[l][...] = dot_nt(eye(K[l]), at(f"oT{l}")[...]).astype(bf)
+
+        def pivot(l, blocks):
+            value = dot_nt(blocks[0], at(f"Z{l}")[0])
+            for r in range(1, R):
+                value = value + dot_nt(blocks[r], at(f"Z{l}")[r])
+            at(f"y{l}")[...] = value.astype(bf)
+
+        start_rhs(3)
+        start_weights(3)
+        start_weights(2)
+        start_rhs(2)
+        make_table(2)
+        wait_rhs(3)
+        wait_inverse(3)
+        pivot(3, [at("B3")[r] for r in range(R)])
+        wait_coupling(3)
+        at("u3")[(c // G[3]) % 2, 0] = (-dot_nt(at("y3")[...], at("C3")[...])).astype(bf)
+        share_update(3)
+        start_weights(1)
+        start_rhs(1)
+        make_table(1)
+
+        for l in (2, 1, 0):
+            wait_update(l + 1)
+            pair = [at(f"u{l + 1}")[child].reshape(N, S[l + 1]) for child in range(2)]
+
+            def assembled(low, size):
+                value = dot_nt(pair[0], at(f"hot{l}")[0, low:low + size, :])
+                return value + dot_nt(pair[1], at(f"hot{l}")[1, low:low + size, :])
+
+            wait_rhs(l)
+            blocks = [
+                (at(f"B{l}")[r].astype(jnp.float32) + assembled(r * K[l], K[l])).astype(bf)
+                for r in range(R)
+            ]
+            wait_inverse(l)
+            pivot(l, blocks)
+            if l:
+                wait_coupling(l)
+                share = (G[l], N // G[l], S[l])
+                at(f"up{l}")[...] = (
+                    dot_nt(at(f"y{l}")[...], at(f"C{l}")[...]).astype(bf).reshape(share)
+                )
+                scatter(f"up{l}", l, f"ut{l}", f"ups{l}", f"upr{l}")
+                if l == 2:
+                    start_weights(0)
+                    start_rhs(0)
+                    make_table(0)
+                at(f"H{l}")[...] = assembled(S[l], S[l]).astype(bf).reshape(share)
+                reduced = total(f"up{l}", l, f"ut{l}", f"upr{l}")
+                q = c % G[l]
+                at(f"u{l}")[(c // G[l]) % 2, q] = (
+                    at(f"H{l}")[q].astype(jnp.float32) - reduced
+                ).astype(bf)
+                share_update(l)
+
+        per = G[0] // R
+        lanes = S[0] // G[0]
+        for r in range(R):
+            value = dot_nn(at("y0")[...], at("Z0")[r]).astype(bf)
+            for i in range(per):
+                at("xp0")[r * per + i] = value[:, i * lanes:(i + 1) * lanes]
+        scatter("xp0", 0, "xr0", "xps0", "xpr0")
+        at("xs0")[c % G[0]] = total("xp0", 0, "xr0", "xpr0").astype(bf)
+        share_solution(0)
+        wait_solution(0)
+        for r in range(R):
+            for i in range(per):
+                at("fx0")[r, :, i * lanes:(i + 1) * lanes] = at("xs0")[r * per + i]
+        start_out(0)
+
+        for l in (1, 2, 3):
+            child = (c // G[l]) % 2
+            gathered = dot_nn(at(f"fx{l - 1}")[0], at(f"hot{l - 1}")[child, 0:K[l - 1], :])
+            for r in range(1, R):
+                gathered = gathered + dot_nn(
+                    at(f"fx{l - 1}")[r],
+                    at(f"hot{l - 1}")[child, r * K[l - 1]:(r + 1) * K[l - 1], :],
+                )
+            if l > 1:
+                gathered = gathered + dot_nn(
+                    at(f"v{l - 1}")[...], at(f"hot{l - 1}")[child, S[l - 1]:, :]
+                )
+            at(f"v{l}")[...] = gathered.astype(bf)
+            residual = (
+                at(f"y{l}")[...].astype(jnp.float32)
+                - dot_nn(at(f"v{l}")[...], at(f"C{l}")[...])
+            ).astype(bf)
+            for r in range(R):
+                value = dot_nn(residual, at(f"Z{l}")[r]).astype(bf)
+                if G[l] > 1:
+                    at(f"xp{l}")[:, r] = value.reshape(G[l], N // G[l], K[l])
+                else:
+                    at(f"fx{l}")[r] = value
+            if G[l] > 1:
+                scatter(f"xp{l}", l, f"xr{l}", f"xps{l}", f"xpr{l}")
+                if l == 1:
+                    finish_out(0)
+                at(f"xs{l}")[c % G[l]] = total(f"xp{l}", l, f"xr{l}", f"xpr{l}").astype(bf)
+                share_solution(l)
+                wait_solution(l)
+                for r in range(R):
+                    at(f"fx{l}")[r] = at(f"xs{l}")[:, r].reshape(N, K[l])
+            start_out(l)
+        for l in (1, 2, 3):
+            finish_out(l)
+        for finish in sent:
+            finish()
+
+    return kernel, scratch
+
+
+def fused_device(*blocks):
+    plan = Plan(
+        lax.axis_size("row"), lax.axis_size("col"),
+        [block.shape for block in blocks[:4]], blocks[7].shape,
+    )
+    if not plan.fits():
+        return per_device(*blocks)
+    kernel, scratch = build_kernel(plan)
+    vmem = pl.BlockSpec(memory_space=pltpu.VMEM)
+    return pl.pallas_call(
+        kernel,
+        out_shape=tuple(jax.ShapeDtypeStruct(block.shape, block.dtype) for block in blocks[7:11]),
+        in_specs=[vmem] * 14,
+        out_specs=(vmem,) * 4,
+        scratch_shapes=scratch,
+        compiler_params=pltpu.CompilerParams(
+            collective_id=0, has_side_effects=True, vmem_limit_bytes=56 * 2**20
+        ),
+    )(*blocks)
+
+
 def solution(mesh):
     in_specs = (
         P("col", "row"),
@@ -228,5 +687,5 @@
     )
     out_specs = (P("row", "col"), P("row", "col"), P("row", "col"), P("row", "col"))
     return jax.shard_map(
-        per_device, mesh=mesh, in_specs=in_specs, out_specs=out_specs, check_vma=False
+        fused_device, mesh=mesh, in_specs=in_specs, out_specs=out_specs, check_vma=False
     )

time: 548 us -> 102 us (0.19)
  waiting for transfers between devices: 312 us -> 0 us
  local copies, waits for them, and re-layouts: 135 us -> 6.61 us
  Pallas kernels: 0 us -> 94.6 us
  blocking collectives: 29.3 us -> 0 us
  starting transfers between devices: 24.2 us -> 0 us
  matrix products: 15.5 us -> 0 us
  other arithmetic: 15.2 us -> 0 us
  between operations: 14.9 us -> 0.66 us
    psum x8 -> x0, waiting for transfers between devices: 274 us -> none  [the longest x4 124 us: per_device(): solved = lax.psum(partial_value.astype(jnp.bfloat16), 'row')]
    scatter x6 -> x0, local copies, waits for them, and re-layouts: 115 us -> none  [the longest x3 67.5 us: route_tables(): lookup.at[source, column_at].set(jnp.where(mine_here, offset, block_len))]
    pallas_call x0 -> x1, Pallas kernels: none -> 94.6 us  [fused_device(): pl.pallas_call(kernel, out_shape=tuple((jax.ShapeDtypeStruct(block.shape,...]
    all_to_all x3 -> x0, blocking collectives: 29.3 us -> none  [per_device(): lax.all_to_all(parent_rows[own_lookup], 'row', split_axis=0, concat_axis=...]
    ppermute x21 -> x0, waiting for transfers between devices: 24.6 us -> none  [swapped(): return lax.ppermute(value, axis, pairs)]
    dot_general x14 -> x0, matrix products: 15.5 us -> none  [the longest x4 5.54 us: per_device(): jnp.dot(inverses[tree_level].T, residual, preferred_element_type=jnp.floa...]
    ppermute x21 -> x0, starting transfers between devices: 13.5 us -> none  [swapped(): return lax.ppermute(value, axis, pairs)]
    all_to_all x3 -> x0, waiting for transfers between devices: 13 us -> none  [per_device(): lax.all_to_all(pack_rows(updated, own_target, own_slots, strips, capacity...]
  transfers between devices with their start and end apart: 32 -> 0, of which waited for: 24 -> 0; matrix products, arithmetic and copies ran while one was open for 26% -> 0% of each run, Pallas kernels for 0% -> 0%
where the time goes in v1:
time: 102 us
  Pallas kernels  94.6 us (93%)
  local copies, waits for them, and re-layouts  6.61 us (6%)
    pallas_call x1, Pallas kernels, fused_device(): pl.pallas_call(kernel, out_shape=tuple((jax.ShapeDtypeStruct(block.shape,...  94.6 us
    unnamed x15, local copies, waits for them, and re-layouts  4.37 us
    pallas_call x2, local copies, waits for them, and re-layouts, fused_device(): pl.pallas_call(kernel, out_shape=tuple((jax.ShapeDtypeStruct(block.shape,...  2.24 us

profile of v1, /device:TPU:0, one launch (start us, length us, event | category | flops | bytes accessed | tf_op | source)
XLA Modules:
  0.0 101.9 jit_solution(3331398772148438566)
XLA Ops:
  0.6 0.0 copy-start.1
  0.6 1.5 %copy.20.refs_8_ = bf16[192,64]{1,0:T(8,128)(2,1)} copy(bf16[192,64]{0,1:T(8,128)(2,1)} %param.22) | data formatting | bytes 49152 | tf_op args[8]
  2.1 0.0 copy-done.1
  2.1 0.0 copy-start.4
  2.1 0.7 copy.18.refs_3_
  2.8 0.0 copy-done.4
  2.9 0.7 copy.19.refs_7_
  3.6 94.6 %shard_map.165 = (bf16[256,32]{1,0:T(8,128)(2,1)}, bf16[192,64]{1,0:T(8,128)(2,1)}, bf16[128,128]{1,0:T(8,128)(2,1)}, bf16[64,256]{1,0:T(8,128)(2,1)}) custom-call(bf16[128,256]{1,0:T(8,128)(2,1)} %refs_0_.1, bf16[192,192]{1,0:T(8,128)(2,1)} %refs_1_.1, bf16[256,128]{1,0:T(8,128)(2,1)} %refs_2_.1, bf16[256,64]{1,0:T(8,128)(2,1)} %copy.18.refs_3_, ...), custom_call_target="tpu_custom_call" | custom-call | tf_op jit(solution)/shard_map/pallas_call | solution.py:659
  98.2 0.0 copy-start
  98.2 1.5 %copy.21 = bf16[256,32]{0,1:T(8,128)(2,1)} copy(bf16[256,32]{1,0:T(8,128)(2,1)} %get-tuple-element.4) | data formatting | bytes 32768 | tf_op jit(solution)/shard_map/pallas_call | solution.py:659
  99.7 0.0 copy-done
  99.7 0.0 copy-start.3
  99.7 0.7 copy.22
  100.4 0.0 copy-done.3
  100.5 0.0 copy-start.2
  100.5 0.6 copy.25
  101.1 0.2 copy-done.2
  101.2 0.6 copy.26
Async XLA Ops:
  0.6 1.5 %copy-start.1 = (bf16[256,64]{0,1:T(8,128)(2,1)S(1)}, bf16[256,64]{0,1:T(8,128)(2,1)}, u32[]{:S(2)}) copy-start(bf16[256,64]{0,1:T(8,128)(2,1)} %param.17) | copy-start | bytes 98308
  2.1 0.7 copy-start.4
  98.2 1.5 %copy-start = (bf16[192,64]{1,0:T(8,128)(2,1)S(1)}, bf16[192,64]{1,0:T(8,128)(2,1)}, u32[]{:S(2)}) copy-start(bf16[192,64]{1,0:T(8,128)(2,1)} %get-tuple-element.5) | copy-start | bytes 73732
  99.7 0.8 copy-start.3
  100.5 0.8 copy-start.2

commit v2 on v1

--- a/solution.py
+++ b/solution.py
@@ -256,7 +256,7 @@
         table = sum(
             2 * self.total(level) * self.order[level + 1] * 2 for level in range(3)
         )
-        if self.group[3] != 1 or self.mine * self.rows != self.columns or table > 24 * 2**20:
+        if self.rows < 3 or self.group[3] != 1 or self.mine * self.rows != self.columns or table > 24 * 2**20:
             return False
         for level in range(4):
             if self.strip[level] % 16 or self.order[level] % 128 or self.width[level] % 16:
@@ -269,6 +269,10 @@
         return self.order[0] % (128 * self.group[0]) == 0 and self.group[0] % self.rows == 0
 
 
+def narrow(size):
+    return size < 128
+
+
 def build_kernel(plan):
     R, CC, N = plan.rows, plan.cols, plan.mine
     S, K, L, G, W = plan.order, plan.strip, plan.local, plan.group, plan.width
@@ -286,17 +290,19 @@
     for l in range(4):
         n_dest = max(1, W[l] // N)
         n_part = max(1, N // W[l])
-        ref(f"Z{l}", (R, L[l], K[l]))
-        sems(f"Zs{l}", (R,))
-        sems(f"Zr{l}", (R,))
+        ref(f"Z{l}", (R, K[l], L[l]) if narrow(K[l]) else (R, L[l], K[l]))
+        sems(f"Zs{l}", (2, R))
+        sems(f"Zr{l}", (2, R))
         if l:
             ref(f"C{l}", (S[l], L[l]))
-            sems(f"Cs{l}", (R,))
-            sems(f"Cr{l}", (R,))
+            sems(f"Cs{l}", (2, R))
+            sems(f"Cr{l}", (2, R))
         ref(f"bT{l}", (W[l], K[l]))
         ref(f"B{l}", (R, N, K[l]))
-        sems(f"Bs{l}", (n_dest, G[l]))
-        sems(f"Br{l}", (R, n_part))
+        sems(f"Bs{l}", (n_dest,))
+        sems(f"Br{l}", (R,))
+        sems(f"Ds{l}", (G[l],))
+        sems(f"Dr{l}", (n_part,))
         ref(f"y{l}", (N, L[l]))
         ref(f"fx{l}", (R, N, K[l]))
         ref(f"oT{l}", (W[l], K[l]))
@@ -372,16 +378,22 @@
             pltpu.make_async_copy(dst, dst, rsem).wait()
 
         barrier = pltpu.get_barrier_semaphore()
-        for dz in range(R):
-            for m in range(CC):
-                if dz or m:
-                    pl.semaphore_signal(
-                        barrier, inc=1, device_id=((z + dz) % R, flipped(c, m)),
-                        device_id_type=MESH,
-                    )
+        for d in range(1, R):
+            pl.semaphore_signal(
+                barrier, inc=1, device_id=((z + d) % R, c), device_id_type=MESH
+            )
+        for m in range(1, CC):
+            pl.semaphore_signal(
+                barrier, inc=1, device_id=(z, flipped(c, m)), device_id_type=MESH
+            )
+        turned = []
         for l in range(4):
-            at(f"bT{l}")[...] = dot_nt(eye(W[l]), rhs[l][...]).astype(bf)
-        pl.semaphore_wait(barrier, R * CC - 1)
+            if narrow(W[l]):
+                turned.append(rhs[l])
+            else:
+                at(f"bT{l}")[...] = dot_nt(eye(W[l]), rhs[l][...]).astype(bf)
+                turned.append(at(f"bT{l}"))
+        pl.semaphore_wait(barrier, R + CC - 2)
 
         def start_rhs(l):
             q = c % G[l]
@@ -389,51 +401,118 @@
             for i in range(n_dest):
                 if W[l] >= N:
                     z_to = q * n_dest + i
-                    src = at(f"bT{l}").at[pl.ds(i * N, N)]
+                    src = turned[l].at[pl.ds(i * N, N)]
                     dst = at(f"B{l}").at[z]
-                    part = 0
                 else:
                     z_to = q // n_part
-                    part = q % n_part
-                    src = at(f"bT{l}")
-                    dst = at(f"B{l}").at[z, pl.ds(pl.multiple_of(part * W[l], W[l]), W[l])]
-                for m in range(G[l]):
-                    ssem, rsem = at(f"Bs{l}").at[i, m], at(f"Br{l}").at[z, part]
-                    if m:
-                        send(src, dst, ssem, rsem, z_to, flipped(c, m))
-                    else:
-                        send_or_copy(src, dst, ssem, rsem, z_to, c, z_to == z)
+                    src = turned[l]
+                    low = pl.multiple_of((q % n_part) * W[l], W[l])
+                    dst = at(f"B{l}").at[z, pl.ds(low, W[l])]
+                ssem, rsem = at(f"Bs{l}").at[i], at(f"Br{l}").at[z]
+                send_or_copy(src, dst, ssem, rsem, z_to, c, z_to == z)
+
+        def rhs_part(l, part):
+            if W[l] >= N:
+                return at(f"B{l}")
+            return at(f"B{l}").at[:, pl.ds(pl.multiple_of(part * W[l], W[l]), W[l])]
+
+        def spread_rhs(l):
+            q = c % G[l]
+            n_dest, n_part = max(1, W[l] // N), max(1, N // W[l])
+            holds = z // n_dest == q // n_part
+            part = q % n_part
+            here = rhs_part(l, part)
+
+            def copy_to(m):
+                return remote(
+                    here, here, at(f"Ds{l}").at[m], at(f"Dr{l}").at[part], z, flipped(c, m)
+                )
+
+            @pl.when(holds)
+            def _():
+                for r in range(R):
+                    block = at(f"B{l}").at[r]
+                    if n_part > 1:
+                        low = pl.multiple_of(part * W[l], W[l])
+                        block = at(f"B{l}").at[r, pl.ds(low, W[l])]
+                    arrived(block, at(f"Br{l}").at[r])
+                for m in range(1, G[l]):
+                    copy_to(m).start()
+
+            def finish():
+                @pl.when(holds)
+                def _():
+                    for m in range(1, G[l]):
+                        copy_to(m).wait_send()
+
+            sent.append(finish)
 
         def wait_rhs(l):
-            n_part = max(1, N // W[l])
-            for s in range(R):
-                for part in range(n_part):
-                    if n_part > 1:
-                        dst = at(f"B{l}").at[s, pl.ds(part * W[l], W[l])]
-                    else:
-                        dst = at(f"B{l}").at[s]
-                    arrived(dst, at(f"Br{l}").at[s, part])
-
-        def c_rows(l, index):
+            q = c % G[l]
+            n_dest, n_part = max(1, W[l] // N), max(1, N // W[l])
+            for part in range(n_part):
+                @pl.when(z // n_dest * n_part + part != q)
+                def _():
+                    arrived(rhs_part(l, part), at(f"Dr{l}").at[part])
+
+        def z_block(l, index):
+            return at(f"Z{l}").at[index]
+
+        def c_block(l, index):
             return at(f"C{l}").at[pl.ds(pl.multiple_of(index * K[l], 16), K[l])]
 
-        def start_weights(l):
-            pltpu.make_async_copy(inverse[l], at(f"Z{l}").at[z], at(f"Zr{l}").at[0]).start()
+        kinds = {"Z": (inverse, z_block), "C": (coupling, c_block)}
+
+        def start_line(kind, l):
+            source, block = kinds[kind]
+            src, dst = source[l], block(l, z)
+            pltpu.make_async_copy(src, dst, at(f"{kind}r{l}").at[0, 0]).start()
+            for way, step in ((0, 1), (1, -1)):
+                go_on(kind, l, way, step, 0, src, z)
+
+        def go_on(kind, l, way, step, d, src, origin):
+            open_end = jnp.logical_and(z + step >= 0, z + step < R)
+            begun = jnp.logical_and(z - d * step >= 0, z - d * step < R)
+            ready = jnp.logical_and(open_end, begun)
+            dst = kinds[kind][1](l, origin)
+
+            def copy():
+                return remote(
+                    src, dst, at(f"{kind}s{l}").at[way, d], at(f"{kind}r{l}").at[way, d + 1],
+                    (z + step + R) % R, c,
+                )
+
+            @pl.when(ready)
+            def _():
+                copy().start()
+
+            def finish():
+                @pl.when(ready)
+                def _():
+                    copy().wait_send()
+
+            sent.append(finish)
+
+        def pass_line(kind, l, d):
+            for way, step in ((0, 1), (1, -1)):
+                origin = (z - d * step + R) % R
+                block = kinds[kind][1](l, origin)
+                begun = jnp.logical_and(z - d * step >= 0, z - d * step < R)
+
+                @pl.when(begun)
+                def _():
+                    arrived(block, at(f"{kind}r{l}").at[way, d])
+
+                if d < R - 1:
+                    go_on(kind, l, way, step, d, block, origin)
+
+        def pass_both(l, d):
+            pass_line("Z", l, d)
             if l:
-                pltpu.make_async_copy(coupling[l], c_rows(l, z), at(f"Cr{l}").at[0]).start()
-            for d in range(1, R):
-                z_to = (z + d) % R
-                send(inverse[l], at(f"Z{l}").at[z], at(f"Zs{l}").at[d], at(f"Zr{l}").at[d], z_to, c)
-                if l:
-                    send(coupling[l], c_rows(l, z), at(f"Cs{l}").at[d], at(f"Cr{l}").at[d], z_to, c)
-
-        def wait_inverse(l):
-            for d in range(R):
-                arrived(at(f"Z{l}").at[(z + R - d) % R], at(f"Zr{l}").at[d])
-
-        def wait_coupling(l):
-            for d in range(R):
-                arrived(c_rows(l, (z + R - d) % R), at(f"Cr{l}").at[d])
+                pass_line("C", l, d)
+
+        def own_line(kind, l):
+            arrived(kinds[kind][1](l, z), at(f"{kind}r{l}").at[0, 0])
 
         def scatter(name, l, landed, ssem, rsem):
             q = c % G[l]
@@ -534,28 +613,46 @@
                     arrived(at(f"oT{l}").at[pl.ds(i * N, N)], at(f"Or{l}").at[i])
             else:
                 arrived(at(f"oT{l}"), at(f"Or{l}").at[0])
-            outs[l][...] = dot_nt(eye(K[l]), at(f"oT{l}")[...]).astype(bf)
+            if narrow(W[l]):
+                outs[l][...] = at(f"oT{l}")[...]
+            else:
+                outs[l][...] = dot_nt(eye(K[l]), at(f"oT{l}")[...]).astype(bf)
 
         def pivot(l, blocks):
-            value = dot_nt(blocks[0], at(f"Z{l}")[0])
+            product = dot_nn if narrow(K[l]) else dot_nt
+            value = product(blocks[0], at(f"Z{l}")[0])
             for r in range(1, R):
-                value = value + dot_nt(blocks[r], at(f"Z{l}")[r])
+                value = value + product(blocks[r], at(f"Z{l}")[r])
             at(f"y{l}")[...] = value.astype(bf)
 
+        start_line("Z", 3)
+        start_line("C", 3)
         start_rhs(3)
-        start_weights(3)
-        start_weights(2)
-        start_rhs(2)
+        start_line("Z", 2)
+        for l in (2, 1, 0):
+            start_rhs(l)
         make_table(2)
-        wait_rhs(3)
-        wait_inverse(3)
+        pass_both(3, 1)
+        start_line("C", 2)
+        for d in range(2, R):
+            pass_both(3, d)
+            if d == 2:
+                pass_both(2, 1)
+                start_line("Z", 1)
+        for l in (2, 1, 0):
+            spread_rhs(l)
+        spread_rhs(3)
+        own_line("Z", 3)
         pivot(3, [at("B3")[r] for r in range(R)])
-        wait_coupling(3)
+        own_line("C", 3)
         at("u3")[(c // G[3]) % 2, 0] = (-dot_nt(at("y3")[...], at("C3")[...])).astype(bf)
         share_update(3)
-        start_weights(1)
-        start_rhs(1)
+        pass_both(2, 2)
+        start_line("C", 1)
+        pass_line("Z", 1, 1)
         make_table(1)
+        for d in range(3, R):
+            pass_both(2, d)
 
         for l in (2, 1, 0):
             wait_update(l + 1)
@@ -570,19 +667,29 @@
                 (at(f"B{l}")[r].astype(jnp.float32) + assembled(r * K[l], K[l])).astype(bf)
                 for r in range(R)
             ]
-            wait_inverse(l)
+            if l == 1:
+                for d in range(3, R):
+                    pass_both(1, d)
+                pass_line("Z", 0, 2)
+            if l == 0:
+                for d in range(3, R):
+                    pass_line("Z", 0, d)
+            own_line("Z", l)
             pivot(l, blocks)
             if l:
-                wait_coupling(l)
+                own_line("C", l)
                 share = (G[l], N // G[l], S[l])
                 at(f"up{l}")[...] = (
                     dot_nt(at(f"y{l}")[...], at(f"C{l}")[...]).astype(bf).reshape(share)
                 )
                 scatter(f"up{l}", l, f"ut{l}", f"ups{l}", f"upr{l}")
                 if l == 2:
-                    start_weights(0)
-                    start_rhs(0)
+                    pass_line("C", 1, 1)
+                    start_line("Z", 0)
+                    pass_line("Z", 1, 2)
                     make_table(0)
+                    pass_line("C", 1, 2)
+                    pass_line("Z", 0, 1)
                 at(f"H{l}")[...] = assembled(S[l], S[l]).astype(bf).reshape(share)
                 reduced = total(f"up{l}", l, f"ut{l}", f"upr{l}")
                 q = c % G[l]
@@ -594,7 +701,8 @@
         per = G[0] // R
         lanes = S[0] // G[0]
         for r in range(R):
-            value = dot_nn(at("y0")[...], at("Z0")[r]).astype(bf)
+            product = dot_nt if narrow(K[0]) else dot_nn
+            value = product(at("y0")[...], at("Z0")[r]).astype(bf)
             for i in range(per):
                 at("xp0")[r * per + i] = value[:, i * lanes:(i + 1) * lanes]
         scatter("xp0", 0, "xr0", "xps0", "xpr0")
@@ -624,7 +732,8 @@
                 - dot_nn(at(f"v{l}")[...], at(f"C{l}")[...])
             ).astype(bf)
             for r in range(R):
-                value = dot_nn(residual, at(f"Z{l}")[r]).astype(bf)
+                product = dot_nt if narrow(K[l]) else dot_nn
+                value = product(residual, at(f"Z{l}")[r]).astype(bf)
                 if G[l] > 1:
                     at(f"xp{l}")[:, r] = value.reshape(G[l], N // G[l], K[l])
                 else:
@@ -655,8 +764,12 @@
     if not plan.fits():
         return per_device(*blocks)
     kernel, scratch = build_kernel(plan)
+    blocks = list(blocks)
+    for at in (0, 1, 2, 3, 7, 8, 9, 10):
+        if narrow(blocks[at].shape[1]):
+            blocks[at] = blocks[at].T
     vmem = pl.BlockSpec(memory_space=pltpu.VMEM)
-    return pl.pallas_call(
+    solved = pl.pallas_call(
         kernel,
         out_shape=tuple(jax.ShapeDtypeStruct(block.shape, block.dtype) for block in blocks[7:11]),
         in_specs=[vmem] * 14,
@@ -666,6 +779,9 @@
             collective_id=0, has_side_effects=True, vmem_limit_bytes=56 * 2**20
         ),
     )(*blocks)
+    return tuple(
+        block.T if narrow(width) else block for block, width in zip(solved, plan.width)
+    )
 
 
 def solution(mesh):

time: 102 us -> 78.7 us (0.77)
  Pallas kernels: 94.6 us -> 74.2 us
  local copies, waits for them, and re-layouts: 6.61 us -> 3.49 us
    pallas_call x1, Pallas kernels: 94.6 us -> 74.2 us  [fused_device(): pl.pallas_call(kernel, out_shape=tuple((jax.ShapeDtypeStruct(block.shape,...]
    pallas_call x2 -> x0, local copies, waits for them, and re-layouts: 2.24 us -> none  [fused_device(): pl.pallas_call(kernel, out_shape=tuple((jax.ShapeDtypeStruct(block.shape,...]
    unnamed x15 -> x10, local copies, waits for them, and re-layouts: 4.37 us -> 3.49 us
where the time goes in v2:
time: 78.7 us; the launch traced here: 78.3 us
  Pallas kernels  74.2 us (94%)
  local copies, waits for them, and re-layouts  3.49 us (4%)
    pallas_call x1, Pallas kernels, fused_device(): pl.pallas_call(kernel, out_shape=tuple((jax.ShapeDtypeStruct(block.shape,...  74.2 us
    unnamed x10, local copies, waits for them, and re-layouts  3.49 us

profile of v2, /device:TPU:0, one launch (start us, length us, event | category | flops | bytes accessed | tf_op | source)
XLA Modules:
  0.0 78.3 jit_solution(3440010240061733233)
XLA Ops:
  0.6 74.2 %shard_map.165 = (bf16[32,256]{1,0:T(8,128)(2,1)}, bf16[64,192]{1,0:T(8,128)(2,1)}, bf16[128,128]{1,0:T(8,128)(2,1)}, bf16[64,256]{1,0:T(8,128)(2,1)}) custom-call(bf16[128,256]{1,0:T(8,128)(2,1)} %refs_0_.1, bf16[192,192]{1,0:T(8,128)(2,1)} %refs_1_.1, bf16[256,128]{1,0:T(8,128)(2,1)} %refs_2_.1, bf16[64,256]{1,0:T(8,128)(2,1)} %bitcast.5, ...), custom_call_target="tpu_custom_call" | custom-call | tf_op jit(solution)/shard_map/pallas_call | solution.py:772
  74.8 0.0 copy-start.2
  74.8 1.3 %copy.22 = bf16[256,32]{0,1:T(8,128)(2,1)} copy(bf16[256,32]{0,1:T(8,128)(2,1)} %bitcast.9) | data formatting | bytes 32768
  76.2 0.0 copy-done.2
  76.2 0.0 copy-start.1
  76.2 0.6 copy.23
  76.8 0.2 copy-done.1
  76.9 0.0 copy-start
  76.9 0.6 copy.24
  77.6 0.2 copy-done
  77.7 0.6 copy.25
Async XLA Ops:
  74.8 1.3 %copy-start.2 = (bf16[64,192]{1,0:T(8,128)(2,1)S(1)}, bf16[64,192]{1,0:T(8,128)(2,1)}, u32[]{:S(2)}) copy-start(bf16[64,192]{1,0:T(8,128)(2,1)} %get-tuple-element.9) | copy-start | bytes 73732
  76.2 0.8 copy-start.1
  76.9 0.8 copy-start

commit v3 on v2

--- a/solution.py
+++ b/solution.py
@@ -739,6 +739,19 @@
                 else:
                     at(f"fx{l}")[r] = value
             if G[l] > 1:
+                if G[l] == 2:
+                    send(
+                        at(f"xp{l}"), at(f"xr{l}"), at(f"xps{l}").at[1], at(f"xpr{l}").at[1],
+                        z, flipped(c, 1),
+                    )
+                    arrived(at(f"xr{l}"), at(f"xpr{l}").at[1])
+                    for r in range(R):
+                        both = at(f"xp{l}")[:, r].astype(jnp.float32) + at(f"xr{l}")[:, r].astype(
+                            jnp.float32
+                        )
+                        at(f"fx{l}")[r] = both.astype(bf).reshape(N, K[l])
+                    start_out(l)
+                    continue
                 scatter(f"xp{l}", l, f"xr{l}", f"xps{l}", f"xpr{l}")
                 if l == 1:
                     finish_out(0)
@@ -754,6 +767,11 @@
             finish()
 
     return kernel, scratch
+
+
+def hand_on(*refs):
+    for source, target in zip(refs[:4], refs[4:]):
+        target[...] = source[...]
 
 
 def fused_device(*blocks):
@@ -779,6 +797,12 @@
             collective_id=0, has_side_effects=True, vmem_limit_bytes=56 * 2**20
         ),
     )(*blocks)
+    solved = pl.pallas_call(
+        hand_on,
+        out_shape=tuple(jax.ShapeDtypeStruct(block.shape, block.dtype) for block in solved),
+        in_specs=[vmem] * 4,
+        out_specs=(vmem,) * 4,
+    )(*solved)
     return tuple(
         block.T if narrow(width) else block for block, width in zip(solved, plan.width)
     )

time: 78.7 us -> 75.7 us (0.962)
  local copies, waits for them, and re-layouts: 3.49 us -> 0 us
    unnamed x10 -> x0, local copies, waits for them, and re-layouts: 3.49 us -> none
    pallas_call x0 -> x1, Pallas kernels: none -> 1.46 us  [fused_device(): pl.pallas_call(hand_on, out_shape=tuple((jax.ShapeDtypeStruct(block.shape...]
    pallas_call x1, Pallas kernels: 74.2 us -> 73.3 us  [fused_device(): pl.pallas_call(kernel, out_shape=tuple((jax.ShapeDtypeStruct(block.shape,...]
where the time goes in v3:
time: 75.7 us; the launch traced here: 75.4 us
  Pallas kernels  74.8 us (99%)
    pallas_call x1, Pallas kernels, fused_device(): pl.pallas_call(kernel, out_shape=tuple((jax.ShapeDtypeStruct(block.shape,...  73.3 us

profile of v3, /device:TPU:0, one launch (start us, length us, event | category | flops | bytes accessed | tf_op | source)
XLA Modules:
  0.0 75.4 jit_solution(17391817290574254589)
XLA Ops:
  0.6 73.3 %shard_map.165 = (bf16[32,256]{1,0:T(8,128)(2,1)}, bf16[64,192]{1,0:T(8,128)(2,1)}, bf16[128,128]{1,0:T(8,128)(2,1)}, bf16[64,256]{1,0:T(8,128)(2,1)}) custom-call(bf16[128,256]{1,0:T(8,128)(2,1)} %refs_0_.1, bf16[192,192]{1,0:T(8,128)(2,1)} %refs_1_.1, bf16[256,128]{1,0:T(8,128)(2,1)} %refs_2_.1, bf16[64,256]{1,0:T(8,128)(2,1)} %bitcast.5, ...), custom_call_target="tpu_custom_call" | custom-call | tf_op jit(solution)/shard_map/pallas_call | solution.py:790
  74.0 1.5 %shard_map.166 = (bf16[32,256]{1,0:T(8,128)(2,1)}, bf16[64,192]{1,0:T(8,128)(2,1)}, bf16[128,128]{1,0:T(8,128)(2,1)}, bf16[64,256]{1,0:T(8,128)(2,1)}) custom-call(bf16[32,256]{1,0:T(8,128)(2,1)} %get-tuple-element.12.refs_0_, bf16[64,192]{1,0:T(8,128)(2,1)} %get-tuple-element.13.refs_1_, bf16[128,128]{1,0:T(8,128)(2,1)} %get-tuple-element.14.refs_2_, ...), custom_call_target="tpu_custom_call" | custom-call | tf_op jit(solution)/shard_map/pallas_call | solution.py:800
